TPU v7x, 512 devices: a whole 4x8x8 slice. The times are simulated.
512 devices in a mesh: dp: 2 (over z_lo), ctx: 64 (over y, x, core), tp: 4 (over z_hi).
Axes of the slice: x: 4, y: 8, z: 8 (z_hi: 4, z_lo: 2; z = z_hi * 2 + z_lo), core: 2. Of those that a mesh axis runs over, the one named last changes fastest.
Arguments:
- queries: bfloat16 [65536, 4096], P(('dp', 'ctx'), 'tp'), parts along dimension 0, may hold values from -6 to 6
- keys: bfloat16 [65536, 4096], P(('dp', 'ctx'), 'tp'), parts along dimension 0, may hold values from -6 to 6
- values: bfloat16 [65536, 4096], P(('dp', 'ctx'), 'tp'), parts along dimension 0, may hold values from -6 to 6
Outputs:
- attended: bfloat16 [65536, 4096], P(('dp', 'ctx'), 'tp'), parts along dimension 0
There are 2 independent parts, one for each index of `dp`. A program takes and returns all parts, laid end to end along the dimension named above; each array names one. Nothing has to cross between parts.
All inputs are finite; a program needn't handle non-finite values.
Results may differ from a plain program's by a relative error of at most 0.0069.
Values may be sent and summed in bfloat16 or wider, within the bound.
A program may use at most 64 MiB of HBM per device.

v0:
```python
import jax
import jax.numpy as jnp
from jax import lax
from jax.sharding import PartitionSpec as P

HEAD_DIM = 128
BLOCK = 128


masked_score = -1e30


def extended(array, sides, width):
    for axis, dim in sides:
        peers, length = (lax.axis_size(axis), array.shape[dim])
        up = [(i, (i + 1) % peers) for i in range(peers - 1)]
        down = [(j, i) for i, j in up]
        last = lax.slice_in_dim(array, length - width, length, axis=dim)
        leading = lax.slice_in_dim(array, 0, width, axis=dim)
        before = lax.ppermute(last, axis, up)
        after = lax.ppermute(leading, axis, down)
        array = jnp.concatenate([before, array, after], axis=dim)
    return array


def partner_2(array, axis, bit):
    return lax.ppermute(array, axis, [(i, i ^ 1 << bit) for i in range(lax.axis_size(axis))])


def pair_mean(source):
    source_shape = source.shape
    paired = source.reshape(
        source_shape[:-2] + (source_shape[-2] // 2, 2, source_shape[-1])
    ).astype(jnp.float32)
    return ((paired[..., 0, :] + paired[..., 1, :]) * 0.5).astype(jnp.bfloat16)


def sibling_blocks(coarse, height, block_rows):
    row_count = coarse.shape[1]
    head_dim = coarse.shape[2]
    groups = coarse.reshape(2, row_count // (2 * block_rows), 2, block_rows, head_dim)[:, :, ::-1]
    swapped = groups.reshape(2, row_count // block_rows, block_rows, head_dim)
    return jnp.repeat(swapped, 2**height, axis=1)


def attend(query_tiles_grouped, key_tiles_grouped, value_tiles_grouped, usable):
    logit_scale_factor = 1.0 / query_tiles_grouped.shape[-1] ** 0.5
    logit_matrix = (
        jnp.einsum(
            "sac,sec->sae",
            query_tiles_grouped,
            key_tiles_grouped,
            preferred_element_type=jnp.float32,
        )
        * logit_scale_factor
    )
    logit_matrix = jnp.where(usable[:, None, :], logit_matrix, masked_score)
    row_peak = jnp.max(logit_matrix, axis=-1, keepdims=True)
    weights = jnp.exp(logit_matrix - row_peak)
    row_total = jnp.sum(weights, axis=-1, keepdims=True)
    rounded_scores = weights.astype(jnp.bfloat16)
    weighted_value_sum = jnp.einsum(
        "zif,zfo->zio", rounded_scores, value_tiles_grouped, preferred_element_type=jnp.float32
    )
    return (weighted_value_sum / row_total).astype(jnp.bfloat16)


def per_device(queries, keys, values):
    tok_rows, width = queries.shape
    head_dim = HEAD_DIM
    heads = width // head_dim
    block_rows = BLOCK
    blocks = tok_rows // block_rows
    local_depth = blocks.bit_length() - 1
    ctx_count = lax.axis_size("ctx")
    depth_ctx = ctx_count.bit_length() - 1
    top_level = depth_ctx + local_depth - 1
    ctx_place = lax.axis_index("ctx")
    stacked = jnp.stack([keys, values])
    padded = extended(stacked, (("ctx", 1),), block_rows)
    local_levels = []
    own_coarse = stacked
    for height in range(1, local_depth + 1):
        own_coarse = pair_mean(own_coarse)
        if height < local_depth:
            local_levels.append((height, own_coarse))
    upper_levels = []
    swap_end = top_level + 1
    for height in range(local_depth, swap_end):
        partner = partner_2(own_coarse, "ctx", height - local_depth)
        upper_levels.append((height, partner))
        if height < top_level:
            is_lower = ctx_place // 2 ** (height - local_depth) % 2 == 0
            merged = jnp.where(
                is_lower,
                jnp.concatenate([own_coarse, partner], axis=1),
                jnp.concatenate([partner, own_coarse], axis=1),
            )
            own_coarse = pair_mean(merged)
    position = (
        ctx_place * tok_rows
        + jnp.arange(blocks, dtype=jnp.int32)[:, None] * block_rows
        + jnp.arange(3 * block_rows, dtype=jnp.int32)[None, :]
        - block_rows
    )
    fine_usable = (position >= 0) & (position < ctx_count * tok_rows)
    usable = jnp.concatenate(
        [fine_usable, jnp.ones((blocks, top_level * block_rows), bool)], axis=1
    )

    def per_head(head, result):

        def columns(source):
            return lax.dynamic_slice_in_dim(source, head * head_dim, head_dim, source.ndim - 1)

        head_rims = columns(padded)
        key_parts = [
            jnp.concatenate(
                [
                    head_rims[:, offset * block_rows : offset * block_rows + tok_rows].reshape(
                        2, blocks, block_rows, head_dim
                    )
                    for offset in range(3)
                ],
                axis=2,
            )
        ]
        height, coarse = local_levels[0]
        key_parts.append(sibling_blocks(columns(coarse), height, block_rows))
        for height, coarse in upper_levels:
            key_parts.append(
                jnp.broadcast_to(columns(coarse)[:, None], (2, blocks, block_rows, head_dim))
            )
        key_value = jnp.concatenate(key_parts, axis=2)
        attended = attend(
            columns(queries).reshape(blocks, block_rows, head_dim),
            key_value[0],
            key_value[1],
            usable,
        )
        return lax.dynamic_update_slice_in_dim(
            result, attended.reshape(tok_rows, head_dim), head * head_dim, 1
        )

    result = jnp.zeros((tok_rows, width), jnp.bfloat16)
    return lax.fori_loop(0, heads, per_head, result)


def solution(mesh):
    return jax.shard_map(
        per_device,
        mesh=mesh,
        in_specs=(P(("dp", "ctx"), "tp"), P(("dp", "ctx"), "tp"), P(("dp", "ctx"), "tp")),
        out_specs=P(("dp", "ctx"), "tp"),
        check_vma=False,
    )
```

profile of v0, /device:TPU:1, one launch (start us, length us, event | category | flops | bytes accessed | tf_op | source)
XLA Modules:
  0.0 204.8 jit_solution(6594166717716116394)
XLA Ops:
  0.0 1.6 stack.18
  2.9 1.9 copy-done
  5.3 1.1 copy.22
  7.1 8.7 %collective-permute-start.2 = (bf16[2,128,1024]{2,0,1:T(2,128)(2,1)S(1)}, bf16[2,128,1024]{2,0,1:T(2,128)(2,1)S(1)}, u32[]{:S(2)}, u32[]{:S(2)}) collective-permute-start(bf16[2,128,1024]{2,0,1:T(2,128)(2,1)S(1)} %fusion.26), channel_id=1, source_target_pairs={{0,4},{4,0},{8,12},{12,8},{16,20},{20,16},{24,28},{28,24},{32,36},... | collective-permute-start | bytes 1572872 | tf_op jit(solution)/shard_map/ppermute | solution.py:27
  15.8 1.5 collective-permute-done.2
  17.4 2.3 %broadcast_select_fusion.4 = bf16[2,256,1024]{2,0,1:T(2,128)(2,1)S(1)} fusion(pred[]{:T(512)S(6)} %eq.21, bf16[2,128,1024]{2,0,1:T(2,128)(2,1)S(1)} %collective-permute-done.2, bf16[2,128,1024]{2,0,1:T(2,128)(2,1)S(1)} %fusion.26), kind=kLoop, calls=%fused_computation.43 | loop fusion | flops 1572864 | bytes 2097153 | tf_op jit(solution)/shard_map/jit(_where)/select_n | solution.py:94
  19.7 1.2 convert.6
  21.6 1.9 collective-permute-start.3
  23.6 13.0 %collective-permute-done.3 = bf16[2,128,1024]{2,0,1:T(2,128)(2,1)S(1)} collective-permute-done((bf16[2,128,1024]{2,0,1:T(2,128)(2,1)S(1)}, bf16[2,128,1024]{2,0,1:T(2,128)(2,1)S(1)}, u32[]{:S(2)}, u32[]{:S(2)}) %collective-permute-start.3) | collective-permute-done | bytes 524320 | tf_op jit(solution)/shard_map/ppermute | solution.py:27
  36.6 2.3 %broadcast_select_fusion.3 = bf16[2,256,1024]{2,0,1:T(2,128)(2,1)S(1)} fusion(pred[]{:T(512)S(6)} %eq.22, bf16[2,128,1024]{2,0,1:T(2,128)(2,1)S(1)} %collective-permute-done.3, bf16[2,128,1024]{2,0,1:T(2,128)(2,1)S(1)} %fusion.27), kind=kLoop, calls=%fused_computation.42 | loop fusion | flops 1572864 | bytes 2097153 | tf_op jit(solution)/shard_map/jit(_where)/select_n | solution.py:94
  38.9 1.2 convert.7
  40.8 2.1 %collective-permute-start.4 = (bf16[2,128,1024]{2,0,1:T(2,128)(2,1)S(1)}, bf16[2,128,1024]{2,0,1:T(2,128)(2,1)S(1)}, u32[]{:S(2)}, u32[]{:S(2)}) collective-permute-start(bf16[2,128,1024]{2,0,1:T(2,128)(2,1)S(1)} %fusion.28), channel_id=1, source_target_pairs={{0,16},{4,20},{8,24},{12,28},{16,0},{20,4},{24,8},{28,12},{32,48},... | collective-permute-start | bytes 1572872 | tf_op jit(solution)/shard_map/ppermute | solution.py:27
  43.0 13.5 %collective-permute-done.4 = bf16[2,128,1024]{2,0,1:T(2,128)(2,1)S(1)} collective-permute-done((bf16[2,128,1024]{2,0,1:T(2,128)(2,1)S(1)}, bf16[2,128,1024]{2,0,1:T(2,128)(2,1)S(1)}, u32[]{:S(2)}, u32[]{:S(2)}) %collective-permute-start.4) | collective-permute-done | bytes 524320 | tf_op jit(solution)/shard_map/ppermute | solution.py:27
  56.5 2.3 %broadcast_select_fusion.2 = bf16[2,256,1024]{2,0,1:T(2,128)(2,1)S(1)} fusion(pred[]{:T(512)S(6)} %eq.23, bf16[2,128,1024]{2,0,1:T(2,128)(2,1)S(1)} %collective-permute-done.4, bf16[2,128,1024]{2,0,1:T(2,128)(2,1)S(1)} %fusion.28), kind=kLoop, calls=%fused_computation.41 | loop fusion | flops 1572864 | bytes 2097153 | tf_op jit(solution)/shard_map/jit(_where)/select_n | solution.py:94
  58.8 1.2 convert.8
  60.7 1.9 collective-permute-start.5
  62.7 11.3 %collective-permute-done.5 = bf16[2,128,1024]{2,0,1:T(2,128)(2,1)S(1)} collective-permute-done((bf16[2,128,1024]{2,0,1:T(2,128)(2,1)S(1)}, bf16[2,128,1024]{2,0,1:T(2,128)(2,1)S(1)}, u32[]{:S(2)}, u32[]{:S(2)}) %collective-permute-start.5) | collective-permute-done | bytes 524320 | tf_op jit(solution)/shard_map/ppermute | solution.py:27
  74.0 2.3 %broadcast_select_fusion.1 = bf16[2,256,1024]{2,0,1:T(2,128)(2,1)S(1)} fusion(pred[]{:T(512)S(6)} %eq.24, bf16[2,128,1024]{2,0,1:T(2,128)(2,1)S(1)} %collective-permute-done.5, bf16[2,128,1024]{2,0,1:T(2,128)(2,1)S(1)} %fusion.29), kind=kLoop, calls=%fused_computation.40 | loop fusion | flops 1572864 | bytes 2097153 | tf_op jit(solution)/shard_map/jit(_where)/select_n | solution.py:94
  76.4 1.2 convert.9
  78.3 1.9 collective-permute-start.6
  80.3 5.3 %collective-permute-start = (bf16[2,128,1024]{2,1,0:T(8,128)(2,1)S(1)}, bf16[2,128,1024]{2,1,0:T(8,128)(2,1)S(1)}, u32[]{:S(2)}, u32[]{:S(2)}) collective-permute-start(bf16[2,128,1024]{2,1,0:T(8,128)(2,1)S(1)} %get-tuple-element.276), channel_id=1, source_target_pairs={{0,4},{4,8},{8,12},{12,16},{16,20},{20,24},{24,28},{28,32},{32,36}... | collective-permute-start | bytes 1572872 | tf_op jit(solution)/shard_map/ppermute | solution.py:20
  85.7 1.9 collective-permute-start.1
  87.7 18.5 %collective-permute-done.6 = bf16[2,128,1024]{2,0,1:T(2,128)(2,1)S(1)} collective-permute-done((bf16[2,128,1024]{2,0,1:T(2,128)(2,1)S(1)}, bf16[2,128,1024]{2,0,1:T(2,128)(2,1)S(1)}, u32[]{:S(2)}, u32[]{:S(2)}) %collective-permute-start.6) | collective-permute-done | bytes 524320 | tf_op jit(solution)/shard_map/ppermute | solution.py:27
  106.2 2.3 %broadcast_select_fusion = bf16[2,256,1024]{2,0,1:T(2,128)(2,1)S(1)} fusion(pred[]{:T(512)S(6)} %eq.25, bf16[2,128,1024]{2,0,1:T(2,128)(2,1)S(1)} %collective-permute-done.6, bf16[2,128,1024]{2,0,1:T(2,128)(2,1)S(1)} %fusion.30), kind=kLoop, calls=%fused_computation.39 | loop fusion | flops 1572864 | bytes 2097153 | tf_op jit(solution)/shard_map/jit(_where)/select_n | solution.py:94
  108.6 1.2 convert.10
  110.5 2.4 %collective-permute-start.7 = (bf16[2,128,1024]{2,0,1:T(2,128)(2,1)S(1)}, bf16[2,128,1024]{2,0,1:T(2,128)(2,1)S(1)}, u32[]{:S(2)}, u32[]{:S(2)}) collective-permute-start(bf16[2,128,1024]{2,0,1:T(2,128)(2,1)S(1)} %fusion.31), channel_id=1, source_target_pairs={{0,128},{4,132},{8,136},{12,140},{16,144},{20,148},{24,152},{28,15... | collective-permute-start | bytes 1572872 | tf_op jit(solution)/shard_map/ppermute | solution.py:27
  112.9 1.5 fusion.37
  115.2 1.5 pad_maximum_fusion
  116.7 21.2 %collective-permute-done.7 = bf16[2,128,1024]{2,0,1:T(2,128)(2,1)S(1)} collective-permute-done((bf16[2,128,1024]{2,0,1:T(2,128)(2,1)S(1)}, bf16[2,128,1024]{2,0,1:T(2,128)(2,1)S(1)}, u32[]{:S(2)}, u32[]{:S(2)}) %collective-permute-start.7) | collective-permute-done | bytes 524320 | tf_op jit(solution)/shard_map/ppermute | solution.py:27
  137.8 1.1 broadcast_in_dim.142
  139.0 65.8 %while.13 = (s32[]{:T(128)}, bf16[512,1024]{1,0:T(8,128)(2,1)}, pred[4,1280]{1,0:T(4,128)(4,1)S(1)}, bf16[512,1024]{1,0:T(8,128)(2,1)}, bf16[2,768,1024]{2,1,0:T...) while((s32[]{:T(128)}, bf16[512,1024]{1,0:T(8,128)(2,1)}, ...), condition=%wide.region_3.4_spmd, body=%wide.region_0.3_spmd.sunk | while | flops 340261888 | bytes 19414288 | solution.py:146
  140.3 1.0 constant_dynamic-slice_fusion.19
  (265 shorter events, 70.4 us)
Async XLA Ops:
  0.0 1.8 copy-start.2
  2.9 1.9 copy-start
  7.1 10.3 %collective-permute-start.2 = (bf16[2,128,1024]{2,0,1:T(2,128)(2,1)S(1)}, bf16[2,128,1024]{2,0,1:T(2,128)(2,1)S(1)}, u32[]{:S(2)}, u32[]{:S(2)}) collective-permute-start(bf16[2,128,1024]{2,0,1:T(2,128)(2,1)S(1)} %fusion.26), channel_id=1, source_target_pairs={{0,4},{4,0},{8,12},{12,8},{16,20},{20,16},{24,28},{28,24},{32,36},... | collective-permute-start | bytes 1572872 | tf_op jit(solution)/shard_map/ppermute | solution.py:27
  17.4 3.6 %copy-start.6 = (bf16[2,128,1024]{2,0,1:T(2,128)(2,1)}, bf16[2,128,1024]{2,0,1:T(2,128)(2,1)S(1)}, u32[]{:S(2)}) copy-start(bf16[2,128,1024]{2,0,1:T(2,128)(2,1)S(1)} %collective-permute-done.2) | copy-start | bytes 1572868
  21.6 15.0 %collective-permute-start.3 = (bf16[2,128,1024]{2,0,1:T(2,128)(2,1)S(1)}, bf16[2,128,1024]{2,0,1:T(2,128)(2,1)S(1)}, u32[]{:S(2)}, u32[]{:S(2)}) collective-permute-start(bf16[2,128,1024]{2,0,1:T(2,128)(2,1)S(1)} %fusion.27), channel_id=1, source_target_pairs={{0,8},{4,12},{8,0},{12,4},{16,24},{20,28},{24,16},{28,20},{32,40},... | collective-permute-start | bytes 1572872 | tf_op jit(solution)/shard_map/ppermute | solution.py:27
  36.6 3.6 %copy-start.7 = (bf16[2,128,1024]{2,0,1:T(2,128)(2,1)}, bf16[2,128,1024]{2,0,1:T(2,128)(2,1)S(1)}, u32[]{:S(2)}) copy-start(bf16[2,128,1024]{2,0,1:T(2,128)(2,1)S(1)} %collective-permute-done.3) | copy-start | bytes 1572868
  40.8 15.7 %collective-permute-start.4 = (bf16[2,128,1024]{2,0,1:T(2,128)(2,1)S(1)}, bf16[2,128,1024]{2,0,1:T(2,128)(2,1)S(1)}, u32[]{:S(2)}, u32[]{:S(2)}) collective-permute-start(bf16[2,128,1024]{2,0,1:T(2,128)(2,1)S(1)} %fusion.28), channel_id=1, source_target_pairs={{0,16},{4,20},{8,24},{12,28},{16,0},{20,4},{24,8},{28,12},{32,48},... | collective-permute-start | bytes 1572872 | tf_op jit(solution)/shard_map/ppermute | solution.py:27
  56.5 3.6 %copy-start.8 = (bf16[2,128,1024]{2,0,1:T(2,128)(2,1)}, bf16[2,128,1024]{2,0,1:T(2,128)(2,1)S(1)}, u32[]{:S(2)}) copy-start(bf16[2,128,1024]{2,0,1:T(2,128)(2,1)S(1)} %collective-permute-done.4) | copy-start | bytes 1572868
  60.7 13.3 %collective-permute-start.5 = (bf16[2,128,1024]{2,0,1:T(2,128)(2,1)S(1)}, bf16[2,128,1024]{2,0,1:T(2,128)(2,1)S(1)}, u32[]{:S(2)}, u32[]{:S(2)}) collective-permute-start(bf16[2,128,1024]{2,0,1:T(2,128)(2,1)S(1)} %fusion.29), channel_id=1, source_target_pairs={{0,32},{4,36},{8,40},{12,44},{16,48},{20,52},{24,56},{28,60},{32,0... | collective-permute-start | bytes 1572872 | tf_op jit(solution)/shard_map/ppermute | solution.py:27
  74.0 3.6 %copy-start.9 = (bf16[2,128,1024]{2,0,1:T(2,128)(2,1)}, bf16[2,128,1024]{2,0,1:T(2,128)(2,1)S(1)}, u32[]{:S(2)}) copy-start(bf16[2,128,1024]{2,0,1:T(2,128)(2,1)S(1)} %collective-permute-done.5) | copy-start | bytes 1572868
  76.4 3.9 %copy-start.4 = (bf16[512,1024]{1,0:T(8,128)(2,1)S(1)}, bf16[512,1024]{1,0:T(8,128)(2,1)}, u32[]{:S(2)}) copy-start(bf16[512,1024]{1,0:T(8,128)(2,1)} %param.6) | copy-start | bytes 3145732
  78.3 27.9 %collective-permute-start.6 = (bf16[2,128,1024]{2,0,1:T(2,128)(2,1)S(1)}, bf16[2,128,1024]{2,0,1:T(2,128)(2,1)S(1)}, u32[]{:S(2)}, u32[]{:S(2)}) collective-permute-start(bf16[2,128,1024]{2,0,1:T(2,128)(2,1)S(1)} %fusion.30), channel_id=1, source_target_pairs={{0,64},{4,68},{8,72},{12,76},{16,80},{20,84},{24,88},{28,92},{32,9... | collective-permute-start | bytes 1572872 | tf_op jit(solution)/shard_map/ppermute | solution.py:27
  80.3 34.0 %collective-permute-start = (bf16[2,128,1024]{2,1,0:T(8,128)(2,1)S(1)}, bf16[2,128,1024]{2,1,0:T(8,128)(2,1)S(1)}, u32[]{:S(2)}, u32[]{:S(2)}) collective-permute-start(bf16[2,128,1024]{2,1,0:T(8,128)(2,1)S(1)} %get-tuple-element.276), channel_id=1, source_target_pairs={{0,4},{4,8},{8,12},{12,16},{16,20},{20,24},{24,28},{28,32},{32,36}... | collective-permute-start | bytes 1572872 | tf_op jit(solution)/shard_map/ppermute | solution.py:20
  85.7 29.5 %collective-permute-start.1 = (bf16[2,128,1024]{2,1,0:T(8,128)(2,1)S(1)}, bf16[2,128,1024]{2,1,0:T(8,128)(2,1)}, u32[]{:S(2)}, u32[]{:S(2)}) collective-permute-start(bf16[2,128,1024]{2,1,0:T(8,128)(2,1)S(1)} %get-tuple-element.277), channel_id=1, source_target_pairs={{4,0},{8,4},{12,8},{16,12},{20,16},{24,20},{28,24},{32,28},{36,32}... | collective-permute-start | bytes 1572872 | tf_op jit(solution)/shard_map/ppermute | solution.py:21
  106.2 3.6 %copy-start.10 = (bf16[2,128,1024]{2,0,1:T(2,128)(2,1)}, bf16[2,128,1024]{2,0,1:T(2,128)(2,1)S(1)}, u32[]{:S(2)}) copy-start(bf16[2,128,1024]{2,0,1:T(2,128)(2,1)S(1)} %collective-permute-done.6) | copy-start | bytes 1572868
  108.5 4.3 %copy-start.1 = (f32[2,256,2,1024]{3,1,2,0:T(8,128)S(1)}, f32[2,256,2,1024]{3,1,2,0:T(8,128)}, u32[]{:S(2)}) copy-start(f32[2,256,2,1024]{3,1,2,0:T(8,128)} %copy-done) | copy-start | bytes 12582916
  110.5 4.7 %copy-start.3 = (bf16[512,1024]{1,0:T(8,128)(2,1)S(1)}, bf16[512,1024]{1,0:T(8,128)(2,1)}, u32[]{:S(2)}) copy-start(bf16[512,1024]{1,0:T(8,128)(2,1)} %param.7) | copy-start | bytes 3145732
  110.5 4.7 %copy-start.5 = (bf16[512,1024]{1,0:T(8,128)(2,1)S(1)}, bf16[512,1024]{1,0:T(8,128)(2,1)}, u32[]{:S(2)}) copy-start(bf16[512,1024]{1,0:T(8,128)(2,1)} %param.6) | copy-start | bytes 3145732
  110.5 27.3 %collective-permute-start.7 = (bf16[2,128,1024]{2,0,1:T(2,128)(2,1)S(1)}, bf16[2,128,1024]{2,0,1:T(2,128)(2,1)S(1)}, u32[]{:S(2)}, u32[]{:S(2)}) collective-permute-start(bf16[2,128,1024]{2,0,1:T(2,128)(2,1)S(1)} %fusion.31), channel_id=1, source_target_pairs={{0,128},{4,132},{8,136},{12,140},{16,144},{20,148},{24,152},{28,15... | collective-permute-start | bytes 1572872 | tf_op jit(solution)/shard_map/ppermute | solution.py:27
  114.4 0.8 copy-start.11
  137.8 1.1 copy-start.12
where the time goes:
time: 207 us; the launch traced here: 205 us
  waiting for transfers between devices  79.1 us (38%)
  local copies, waits for them, and re-layouts  57.5 us (28%)
  other arithmetic  30 us (14%)
  starting transfers between devices  26.2 us (13%)
  matrix products  10.1 us (5%)
    ppermute x6, waiting for transfers between devices, partner_2(): lax.ppermute(array, axis, [(i, i ^ 1 << bit) for i in range(lax.axis_size...  79.1 us
    dynamic_slice x88, local copies, waits for them, and re-layouts, columns(): lax.dynamic_slice_in_dim(source, head * head_dim, head_dim, source.ndim - 1)  38.6 us
    ppermute x6, starting transfers between devices, partner_2(): lax.ppermute(array, axis, [(i, i ^ 1 << bit) for i in range(lax.axis_size...  19 us
    select_n x5, other arithmetic, per_device(): jnp.where(is_lower, jnp.concatenate([own_coarse, partner], axis=1), jnp.c...  11.6 us
    convert_element_type x6, other arithmetic, pair_mean(): paired = source.reshape(source_shape[:-2] + (source_shape[-2] // 2, 2, so...  6.31 us
    convert_element_type x8, other arithmetic, pair_mean(): return ((paired[..., 0, :] + paired[..., 1, :]) * 0.5).astype(jnp.bfloat16)  6.09 us
    dynamic_update_slice x8, local copies, waits for them, and re-layouts, per_head(): lax.dynamic_update_slice_in_dim(result, attended.reshape(tok_rows, head_d...  5.36 us
    ppermute x1, starting transfers between devices, extended(): before = lax.ppermute(last, axis, up)  5.31 us
  transfers between devices with their start and end apart: 8, of which 6 were waited for; matrix products, arithmetic and copies ran while one was open for 4% of the time, Pallas kernels for 0%

commit v1 on v0

v1 whole, which is shorter than its diff:
```python
import functools
import math

import jax
import jax.numpy as jnp
from jax import lax
from jax.experimental import pallas as pl
from jax.experimental.pallas import tpu as pltpu
from jax.sharding import PartitionSpec as P

HEAD_DIM = 128
BLOCK = 128
ROWS = 512
CTX = 64
PACK = 48
MASKED = -1.0e30
LOG2E = 1.4426950408889634

F32 = jnp.float32
BF16 = jnp.bfloat16

HALO = 0
LEVEL2 = 4
LEVEL3 = 5
LEVEL4 = 6
LEVEL5 = 8
LEVEL6 = 9
LEVEL7 = 11
ALONG_X = 15
HALF34 = 18
SHARE = 19
COPIES = 23


def flip(place, mask):
    bit = 1
    while bit <= mask:
        if mask & bit:
            place = place + bit * (1 - 2 * lax.rem(lax.div(place, bit), 2))
        bit *= 2
    return place


def averaging(rows, cols):
    row = lax.broadcasted_iota(jnp.int32, (rows, cols), 0)
    col = lax.broadcasted_iota(jnp.int32, (rows, cols), 1)
    hit = (col == 2 * row) | (col == 2 * row + 1)
    return jnp.where(hit, 0.5, 0.0).astype(BF16)


def pair_mean(source, rows=None):
    rows = source.shape[0] // 2 if rows is None else rows
    weights = averaging(rows, source.shape[0])
    return jnp.dot(weights, source, preferred_element_type=F32).astype(BF16)


def kernel(
    q_ref, k_ref, v_ref, o_ref,
    halo, c1, c2, c3, c4, c5, c6, c7, far2, far34, got6, got7, far567,
    acc, peak, total, send_sem, recv_sem,
):
    heads = q_ref.shape[1] // HEAD_DIM
    scale = LOG2E / math.sqrt(HEAD_DIM)
    me = lax.axis_index("ctx")
    core = lax.rem(me, 2)
    x = lax.rem(lax.div(me, 2), 4)
    up = lax.rem(me + 1, CTX)
    down = lax.rem(me + CTX - 1, CTX)

    barrier = pltpu.get_barrier_semaphore()
    peers = [up, down] + [flip(me, mask) for mask in (1, 2, 4, 6, 8, 16, 24, 32, 40, 48, 56)]
    for peer in peers:
        pl.semaphore_signal(
            barrier, inc=1, device_id={"ctx": peer}, device_id_type=pl.DeviceIdType.MESH
        )

    def copy(number, source, target, device):
        return pltpu.make_async_remote_copy(
            src_ref=source,
            dst_ref=target,
            send_sem=send_sem.at[number],
            recv_sem=recv_sem.at[number],
            device_id={"ctx": device},
            device_id_type=pl.DeviceIdType.MESH,
        )

    for which, ref in ((0, k_ref), (1, v_ref)):
        for half in range(2):
            c1[which, half * 128:(half + 1) * 128] = pair_mean(ref[half * 256:(half + 1) * 256])
        c2[which] = pair_mean(c1[which])
        c3[which] = pair_mean(c2[which])
        c4[which] = pair_mean(c3[which])
        c5[which] = pair_mean(c4[which])
    c6[...] = pair_mean(c5[...].reshape(32, c5.shape[2]))
    c7[...] = pair_mean(c6[...], 16)

    pl.semaphore_wait(barrier, len(peers))

    copies = {}
    copies[LEVEL5] = copy(LEVEL5, c5, far567.at[:, core, x, pl.ds(0, 16)], flip(me, 8))
    for j in range(2):
        copies[LEVEL6 + j] = copy(LEVEL6 + j, c6, got6.at[j], flip(me, 16 + 8 * j))
    for j in range(4):
        copies[LEVEL7 + j] = copy(LEVEL7 + j, c7, got7.at[j], flip(me, 32 + 8 * j))
    last, first = pl.ds(ROWS - BLOCK, BLOCK), pl.ds(0, BLOCK)
    copies[HALO] = copy(HALO, k_ref.at[last], halo.at[0, 0], up)
    copies[HALO + 1] = copy(HALO + 1, v_ref.at[last], halo.at[1, 0], up)
    copies[HALO + 2] = copy(HALO + 2, k_ref.at[first], halo.at[0, 1], down)
    copies[HALO + 3] = copy(HALO + 3, v_ref.at[first], halo.at[1, 1], down)
    copies[LEVEL2] = copy(LEVEL2, c2, far2, flip(me, 1))
    copies[LEVEL3] = copy(LEVEL3, c3, far34.at[:, core, pl.ds(0, 64)], flip(me, 2))
    for j in range(2):
        copies[LEVEL4 + j] = copy(
            LEVEL4 + j, c4, far34.at[:, core, pl.ds(64 + 32 * j, 32)], flip(me, 4 + 2 * j)
        )
    for item in copies.values():
        item.start()

    def attend(head, row, rows, keys, values, first=False, last=False, valid=None):
        lanes = pl.ds(pl.multiple_of(head * HEAD_DIM, HEAD_DIM), HEAD_DIM)
        span = pl.ds(row, rows)
        count = keys.shape[0]
        scores = lax.dot_general(
            q_ref[span, lanes], keys, (((1,), (1,)), ((), ())), preferred_element_type=F32
        )
        if valid is not None:
            edge = jnp.where(valid, scores[:, :BLOCK], MASKED)
            scores = jnp.concatenate([edge, scores[:, BLOCK:]], axis=1)
        top = jnp.max(scores, axis=1, keepdims=True)
        if first:
            new = jnp.broadcast_to(top, (rows, 128))
        else:
            old = peak[head, span]
            new = jnp.maximum(old, top)
            fade = jnp.exp2((old - new) * scale)
        wide = jnp.concatenate([new] * (count // 128), axis=1)
        weights = jnp.exp2((scores - wide) * scale).astype(BF16)
        ones = jnp.ones((count, 128), BF16)
        both = jnp.dot(
            weights, jnp.concatenate([values, ones], axis=1), preferred_element_type=F32
        )
        part, part_total = both[:, :128], both[:, 128:]
        if not first:
            part = acc[head, span] * fade + part
            part_total = total[head, span] * fade + part_total
        if last:
            o_ref[span, lanes] = (part / part_total).astype(BF16)
        else:
            acc[head, span] = part
            total[head, span] = part_total
            peak[head, span] = new

    def lanes_of(head):
        return pl.ds(pl.multiple_of(head * HEAD_DIM, HEAD_DIM), HEAD_DIM)

    def own(head, carry):
        lanes = lanes_of(head)
        for block in range(4):
            low, high = max(block - 1, 0) * BLOCK, min(block + 2, 4) * BLOCK
            side = pl.ds(128 if block < 2 else 0, 128)
            keys = jnp.concatenate([k_ref[low:high, lanes], c1[0, side, lanes]], axis=0)
            values = jnp.concatenate([v_ref[low:high, lanes], c1[1, side, lanes]], axis=0)
            attend(head, block * BLOCK, BLOCK, keys, values, first=True)
        return carry

    lax.fori_loop(0, heads, own, 0)

    for number in range(LEVEL5, LEVEL7 + 4):
        copies[number].wait_recv()
    for which in range(2):
        rows6 = [got6[j, 8 * which:8 * which + 8].astype(F32) for j in range(2)]
        rows7 = [got7[j, 0:8].astype(F32)[4 * which:4 * which + 4] for j in range(4)]
        far567[which, core, x, 16:32] = jnp.concatenate(rows6, axis=0).astype(BF16)
        far567[which, core, x, 32:48] = jnp.concatenate(rows7, axis=0).astype(BF16)
    mine = far567.at[:, core, x]
    for j in range(1, 4):
        copies[ALONG_X + j - 1] = copy(ALONG_X + j - 1, mine, mine, flip(me, 2 * j))
        copies[ALONG_X + j - 1].start()
    copies[SHARE] = copy(SHARE, mine, mine, flip(me, 1))
    copies[SHARE].start()

    for number in (LEVEL3, LEVEL4, LEVEL4 + 1):
        copies[number].wait_recv()
    half = far34.at[:, core]
    copies[HALF34] = copy(HALF34, half, half, flip(me, 1))
    copies[HALF34].start()

    for number in range(HALO, LEVEL2 + 1):
        copies[number].wait_recv()

    def near(head, carry):
        lanes = lanes_of(head)
        keys2, values2 = far2[0, :, lanes], far2[1, :, lanes]
        for side, row, valid in ((0, 0, me > 0), (1, 3 * BLOCK, me < CTX - 1)):
            keys = jnp.concatenate([halo[0, side, :, lanes], keys2], axis=0)
            values = jnp.concatenate([halo[1, side, :, lanes], values2], axis=0)
            attend(head, row, BLOCK, keys, values, valid=valid)
        attend(head, BLOCK, 2 * BLOCK, keys2, values2)
        return carry

    lax.fori_loop(0, heads, near, 0)

    for j in range(1, 4):
        copies[ALONG_X + j - 1].wait_recv()
        came = far567.at[:, core, flip(x, j)]
        copies[SHARE + j] = copy(SHARE + j, came, came, flip(me, 1))
        copies[SHARE + j].start()

    copies[HALF34].wait_recv()

    def middle(head, carry):
        lanes = lanes_of(head)
        keys = far34[0, :, :, lanes].reshape(256, HEAD_DIM)
        values = far34[1, :, :, lanes].reshape(256, HEAD_DIM)
        for part in range(2):
            attend(head, part * 256, 256, keys, values)
        return carry

    lax.fori_loop(0, heads, middle, 0)

    for j in range(4):
        copies[SHARE + j].wait_recv()

    def distant(head, carry):
        lanes = lanes_of(head)
        keys = far567[0, :, :, :, lanes].reshape(8 * PACK, HEAD_DIM)
        values = far567[1, :, :, :, lanes].reshape(8 * PACK, HEAD_DIM)
        for part in range(2):
            attend(head, part * 256, 256, keys, values, last=True)
        return carry

    lax.fori_loop(0, heads, distant, 0)

    for item in copies.values():
        item.wait_send()


def per_device(queries, keys, values):
    rows, width = queries.shape
    heads = width // HEAD_DIM
    state = pltpu.VMEM((heads, rows, 128), F32)
    return pl.pallas_call(
        kernel,
        out_shape=jax.ShapeDtypeStruct((rows, width), BF16),
        in_specs=[pl.BlockSpec(memory_space=pltpu.VMEM)] * 3,
        out_specs=pl.BlockSpec(memory_space=pltpu.VMEM),
        scratch_shapes=[
            pltpu.VMEM((2, 2, BLOCK, width), BF16),
            pltpu.VMEM((2, 256, width), BF16),
            pltpu.VMEM((2, 128, width), BF16),
            pltpu.VMEM((2, 64, width), BF16),
            pltpu.VMEM((2, 32, width), BF16),
            pltpu.VMEM((2, 16, width), BF16),
            pltpu.VMEM((16, width), BF16),
            pltpu.VMEM((16, width), BF16),
            pltpu.VMEM((2, 128, width), BF16),
            pltpu.VMEM((2, 2, 128, width), BF16),
            pltpu.VMEM((2, 16, width), BF16),
            pltpu.VMEM((4, 16, width), BF16),
            pltpu.VMEM((2, 2, 4, PACK, width), BF16),
            state, state, state,
            pltpu.SemaphoreType.DMA((COPIES,)),
            pltpu.SemaphoreType.DMA((COPIES,)),
        ],
        compiler_params=pltpu.CompilerParams(
            collective_id=0, has_side_effects=True, vmem_limit_bytes=48 * 1024 * 1024
        ),
        name="hierarchical_attention",
    )(queries, keys, values)


def solution(mesh):
    return jax.shard_map(
        per_device,
        mesh=mesh,
        in_specs=(P(("dp", "ctx"), "tp"), P(("dp", "ctx"), "tp"), P(("dp", "ctx"), "tp")),
        out_specs=P(("dp", "ctx"), "tp"),
        check_vma=False,
    )
```

time: 207 us -> 48.3 us (0.23)
  waiting for transfers between devices: 79.1 us -> 0 us
  local copies, waits for them, and re-layouts: 57.5 us -> 4.65 us
  Pallas kernels: 0 us -> 43.4 us
  other arithmetic: 30 us -> 0 us
  starting transfers between devices: 26.2 us -> 0 us
  matrix products: 10.1 us -> 0 us
    ppermute x8 -> x0, waiting for transfers between devices: 79.1 us -> none  [the longest x6 79.1 us: partner_2(): lax.ppermute(array, axis, [(i, i ^ 1 << bit) for i in range(lax.axis_size...]
    pallas_call x0 -> x1, Pallas kernels: none -> 43.4 us  [per_device(): pl.pallas_call(kernel, out_shape=jax.ShapeDtypeStruct((rows, width), BF16...]
    dynamic_slice x88 -> x0, local copies, waits for them, and re-layouts: 38.6 us -> none  [columns(): lax.dynamic_slice_in_dim(source, head * head_dim, head_dim, source.ndim - 1)]
    ppermute x8 -> x0, starting transfers between devices: 26.2 us -> none  [the longest x6 19 us: partner_2(): lax.ppermute(array, axis, [(i, i ^ 1 << bit) for i in range(lax.axis_size...]
    convert_element_type x14 -> x0, other arithmetic: 12.4 us -> none  [the longest x6 6.31 us: pair_mean(): paired = source.reshape(source_shape[:-2] + (source_shape[-2] // 2, 2, so...]
    select_n x5 -> x0, other arithmetic: 11.6 us -> none  [per_device(): jnp.where(is_lower, jnp.concatenate([own_coarse, partner], axis=1), jnp.c...]
    dot_general x16 -> x0, matrix products: 10.1 us -> none  [the longest x8 5.2 us: attend(): jnp.einsum('zif,zfo->zio', rounded_scores, value_tiles_grouped, preferred...]
    dynamic_update_slice x8 -> x0, local copies, waits for them, and re-layouts: 5.36 us -> none  [per_head(): lax.dynamic_update_slice_in_dim(result, attended.reshape(tok_rows, head_d...]
  transfers between devices with their start and end apart: 8 -> 0, of which waited for: 6 -> 0; matrix products, arithmetic and copies ran while one was open for 4% -> 0% of each run, Pallas kernels for 0% -> 0%
where the time goes in v1:
time: 48.3 us; the launch traced here: 48.1 us
  Pallas kernels  43.4 us (90%)
  local copies, waits for them, and re-layouts  4.65 us (10%)
    pallas_call x1, Pallas kernels, per_device(): pl.pallas_call(kernel, out_shape=jax.ShapeDtypeStruct((rows, width), BF16...  43.4 us
    unnamed x7, local copies, waits for them, and re-layouts  4.65 us

profile of v1, /device:TPU:1, one launch (start us, length us, event | category | flops | bytes accessed | tf_op | source)
XLA Modules:
  0.0 48.1 jit_solution(9954222240064409968)
XLA Ops:
  0.0 0.0 copy-start
  0.0 1.2 %copy-done = bf16[512,1024]{1,0:T(8,128)(2,1)S(1)} copy-done((bf16[512,1024]{1,0:T(8,128)(2,1)S(1)}, bf16[512,1024]{1,0:T(8,128)(2,1)}, u32[]{:S(2)}) %copy-start) | copy-done | bytes 1048600
  1.2 0.0 copy-start.1
  1.2 1.2 %copy-done.1 = bf16[512,1024]{1,0:T(8,128)(2,1)S(1)} copy-done((bf16[512,1024]{1,0:T(8,128)(2,1)S(1)}, bf16[512,1024]{1,0:T(8,128)(2,1)}, u32[]{:S(2)}) %copy-start.1) | copy-done | bytes 1048600
  2.5 0.0 copy-start.2
  2.5 1.2 %copy-done.2 = bf16[512,1024]{1,0:T(8,128)(2,1)S(1)} copy-done((bf16[512,1024]{1,0:T(8,128)(2,1)S(1)}, bf16[512,1024]{1,0:T(8,128)(2,1)}, u32[]{:S(2)}) %copy-start.2) | copy-done | bytes 1048600
  3.7 43.4 %hierarchical_attention.1 = bf16[512,1024]{1,0:T(8,128)(2,1)S(1)} custom-call(bf16[512,1024]{1,0:T(8,128)(2,1)S(1)} %copy-done, bf16[512,1024]{1,0:T(8,128)(2,1)S(1)} %copy-done.1, bf16[512,1024]{1,0:T(8,128)(2,1)S(1)} %copy-done.2), custom_call_target="tpu_custom_call" | custom-call | tf_op jit(solution)/shard_map/hierarchical_attention/pallas_call | solution.py:242
  47.1 1.0 %copy.5 = bf16[512,1024]{1,0:T(8,128)(2,1)} copy(bf16[512,1024]{1,0:T(8,128)(2,1)S(1)} %hierarchical_attention.1) | data formatting | bytes 2097152
Async XLA Ops:
  0.0 1.2 %copy-start = (bf16[512,1024]{1,0:T(8,128)(2,1)S(1)}, bf16[512,1024]{1,0:T(8,128)(2,1)}, u32[]{:S(2)}) copy-start(bf16[512,1024]{1,0:T(8,128)(2,1)} %q_ref.1) | copy-start | bytes 3145732
  1.2 1.2 %copy-start.1 = (bf16[512,1024]{1,0:T(8,128)(2,1)S(1)}, bf16[512,1024]{1,0:T(8,128)(2,1)}, u32[]{:S(2)}) copy-start(bf16[512,1024]{1,0:T(8,128)(2,1)} %k_ref.1) | copy-start | bytes 3145732
  2.5 1.2 %copy-start.2 = (bf16[512,1024]{1,0:T(8,128)(2,1)S(1)}, bf16[512,1024]{1,0:T(8,128)(2,1)}, u32[]{:S(2)}) copy-start(bf16[512,1024]{1,0:T(8,128)(2,1)} %v_ref.1) | copy-start | bytes 3145732

commit v2 on v1

--- a/solution.py
+++ b/solution.py
@@ -22,14 +22,15 @@
 HALO = 0
 LEVEL2 = 4
 LEVEL3 = 5
-LEVEL4 = 6
-LEVEL5 = 8
-LEVEL6 = 9
-LEVEL7 = 11
-ALONG_X = 15
-HALF34 = 18
-SHARE = 19
-COPIES = 23
+LEVEL4 = 7
+LEVEL5 = 9
+LEVEL6 = 10
+LEVEL7 = 12
+ALONG_X = 16
+SHARE4 = 19
+SHARE3 = 21
+SHARE = 22
+COPIES = 26
 
 
 def flip(place, mask):
@@ -55,9 +56,9 @@
 
 
 def kernel(
-    q_ref, k_ref, v_ref, o_ref,
-    halo, c1, c2, c3, c4, c5, c6, c7, far2, far34, got6, got7, far567,
-    acc, peak, total, send_sem, recv_sem,
+    q_hbm, k_hbm, v_hbm, o_ref, q_ref, k_ref, v_ref,
+    halo, c1, c2, c3, c4, c5, c6, c7, far2, far3, far4, got6, got7, far567,
+    acc, peak, total, send_sem, recv_sem, load_sem,
 ):
     heads = q_ref.shape[1] // HEAD_DIM
     scale = LOG2E / math.sqrt(HEAD_DIM)
@@ -67,6 +68,13 @@
     up = lax.rem(me + 1, CTX)
     down = lax.rem(me + CTX - 1, CTX)
 
+    loads = [
+        pltpu.make_async_copy(source, target, load_sem.at[number])
+        for number, (source, target) in enumerate(((k_hbm, k_ref), (v_hbm, v_ref), (q_hbm, q_ref)))
+    ]
+    for load in loads:
+        load.start()
+
     barrier = pltpu.get_barrier_semaphore()
     peers = [up, down] + [flip(me, mask) for mask in (1, 2, 4, 6, 8, 16, 24, 32, 40, 48, 56)]
     for peer in peers:
@@ -85,6 +93,7 @@
         )
 
     for which, ref in ((0, k_ref), (1, v_ref)):
+        loads[which].wait()
         for half in range(2):
             c1[which, half * 128:(half + 1) * 128] = pair_mean(ref[half * 256:(half + 1) * 256])
         c2[which] = pair_mean(c1[which])
@@ -96,25 +105,27 @@
 
     pl.semaphore_wait(barrier, len(peers))
 
+    side_a, side_b = flip(me, 2), flip(me, 6)
+    twin = flip(me, 1)
     copies = {}
-    copies[LEVEL5] = copy(LEVEL5, c5, far567.at[:, core, x, pl.ds(0, 16)], flip(me, 8))
+
+    def send(number, source, target, device):
+        copies[number] = copy(number, source, target, device)
+        copies[number].start()
+
+    send(LEVEL5, c5, far567.at[:, core, x, pl.ds(0, 16)], flip(me, 8))
     for j in range(2):
-        copies[LEVEL6 + j] = copy(LEVEL6 + j, c6, got6.at[j], flip(me, 16 + 8 * j))
+        send(LEVEL6 + j, c6, got6.at[j], flip(me, 16 + 8 * j))
     for j in range(4):
-        copies[LEVEL7 + j] = copy(LEVEL7 + j, c7, got7.at[j], flip(me, 32 + 8 * j))
-    last, first = pl.ds(ROWS - BLOCK, BLOCK), pl.ds(0, BLOCK)
-    copies[HALO] = copy(HALO, k_ref.at[last], halo.at[0, 0], up)
-    copies[HALO + 1] = copy(HALO + 1, v_ref.at[last], halo.at[1, 0], up)
-    copies[HALO + 2] = copy(HALO + 2, k_ref.at[first], halo.at[0, 1], down)
-    copies[HALO + 3] = copy(HALO + 3, v_ref.at[first], halo.at[1, 1], down)
-    copies[LEVEL2] = copy(LEVEL2, c2, far2, flip(me, 1))
-    copies[LEVEL3] = copy(LEVEL3, c3, far34.at[:, core, pl.ds(0, 64)], flip(me, 2))
-    for j in range(2):
-        copies[LEVEL4 + j] = copy(
-            LEVEL4 + j, c4, far34.at[:, core, pl.ds(64 + 32 * j, 32)], flip(me, 4 + 2 * j)
-        )
-    for item in copies.values():
-        item.start()
+        send(LEVEL7 + j, c7, got7.at[j], flip(me, 32 + 8 * j))
+    send(LEVEL4, c4, far4.at[:, core, 0], side_b)
+    head_rows, tail_rows = pl.ds(0, BLOCK), pl.ds(ROWS - BLOCK, BLOCK)
+    send(HALO, k_hbm.at[tail_rows], halo.at[0, 0], up)
+    send(HALO + 1, v_hbm.at[tail_rows], halo.at[1, 0], up)
+    send(HALO + 2, k_hbm.at[head_rows], halo.at[0, 1], down)
+    send(HALO + 3, v_hbm.at[head_rows], halo.at[1, 1], down)
+    send(LEVEL2, c2, far2, twin)
+    send(LEVEL3, c3.at[0], far3.at[0, core], side_a)
 
     def attend(head, row, rows, keys, values, first=False, last=False, valid=None):
         lanes = pl.ds(pl.multiple_of(head * HEAD_DIM, HEAD_DIM), HEAD_DIM)
@@ -163,6 +174,7 @@
             attend(head, block * BLOCK, BLOCK, keys, values, first=True)
         return carry
 
+    loads[2].wait()
     lax.fori_loop(0, heads, own, 0)
 
     for number in range(LEVEL5, LEVEL7 + 4):
@@ -172,18 +184,16 @@
         rows7 = [got7[j, 0:8].astype(F32)[4 * which:4 * which + 4] for j in range(4)]
         far567[which, core, x, 16:32] = jnp.concatenate(rows6, axis=0).astype(BF16)
         far567[which, core, x, 32:48] = jnp.concatenate(rows7, axis=0).astype(BF16)
-    mine = far567.at[:, core, x]
-    for j in range(1, 4):
-        copies[ALONG_X + j - 1] = copy(ALONG_X + j - 1, mine, mine, flip(me, 2 * j))
-        copies[ALONG_X + j - 1].start()
-    copies[SHARE] = copy(SHARE, mine, mine, flip(me, 1))
-    copies[SHARE].start()
-
-    for number in (LEVEL3, LEVEL4, LEVEL4 + 1):
-        copies[number].wait_recv()
-    half = far34.at[:, core]
-    copies[HALF34] = copy(HALF34, half, half, flip(me, 1))
-    copies[HALF34].start()
+    def pack(place):
+        return far567.at[:, core, place]
+
+    send(ALONG_X, pack(x), pack(x), side_a)
+    send(ALONG_X + 1, pack(x), pack(x), side_b)
+    send(SHARE, pack(x), pack(x), twin)
+    copies[LEVEL4].wait_recv()
+    send(LEVEL4 + 1, far4.at[:, core, 0], far4.at[:, core, 1], side_a)
+    send(SHARE4, far4.at[:, core, 0], far4.at[:, core, 0], twin)
+    send(LEVEL3 + 1, c3.at[1], far3.at[1, core], side_a)
 
     for number in range(HALO, LEVEL2 + 1):
         copies[number].wait_recv()
@@ -200,36 +210,50 @@
 
     lax.fori_loop(0, heads, near, 0)
 
-    for j in range(1, 4):
-        copies[ALONG_X + j - 1].wait_recv()
-        came = far567.at[:, core, flip(x, j)]
-        copies[SHARE + j] = copy(SHARE + j, came, came, flip(me, 1))
-        copies[SHARE + j].start()
-
-    copies[HALF34].wait_recv()
-
-    def middle(head, carry):
+    xa, xb, xc = flip(x, 1), flip(x, 3), flip(x, 2)
+    copies[ALONG_X].wait_recv()
+    send(ALONG_X + 2, pack(xa), pack(xa), side_b)
+    send(SHARE + 1, pack(xa), pack(xa), twin)
+    copies[ALONG_X + 1].wait_recv()
+    send(SHARE + 2, pack(xb), pack(xb), twin)
+    copies[LEVEL4 + 1].wait_recv()
+    send(SHARE4 + 1, far4.at[:, core, 1], far4.at[:, core, 1], twin)
+    copies[ALONG_X + 2].wait_recv()
+    send(SHARE + 3, pack(xc), pack(xc), twin)
+    for number in (LEVEL3, LEVEL3 + 1):
+        copies[number].wait_recv()
+    send(SHARE3, far3.at[:, core], far3.at[:, core], twin)
+    for number in (SHARE4, SHARE4 + 1, SHARE, SHARE + 1, SHARE + 2, SHARE + 3):
+        copies[number].wait_recv()
+
+    def distant(head, carry):
         lanes = lanes_of(head)
-        keys = far34[0, :, :, lanes].reshape(256, HEAD_DIM)
-        values = far34[1, :, :, lanes].reshape(256, HEAD_DIM)
+        keys, values = (
+            jnp.concatenate(
+                [
+                    far567[which, :, :, :, lanes].reshape(8 * PACK, HEAD_DIM),
+                    far4[which, :, :, :, lanes].reshape(128, HEAD_DIM),
+                ],
+                axis=0,
+            )
+            for which in range(2)
+        )
         for part in range(2):
             attend(head, part * 256, 256, keys, values)
         return carry
 
-    lax.fori_loop(0, heads, middle, 0)
-
-    for j in range(4):
-        copies[SHARE + j].wait_recv()
-
-    def distant(head, carry):
+    lax.fori_loop(0, heads, distant, 0)
+
+    copies[SHARE3].wait_recv()
+
+    def level3(head, carry):
         lanes = lanes_of(head)
-        keys = far567[0, :, :, :, lanes].reshape(8 * PACK, HEAD_DIM)
-        values = far567[1, :, :, :, lanes].reshape(8 * PACK, HEAD_DIM)
-        for part in range(2):
-            attend(head, part * 256, 256, keys, values, last=True)
+        keys = far3[0, :, :, lanes].reshape(128, HEAD_DIM)
+        values = far3[1, :, :, lanes].reshape(128, HEAD_DIM)
+        attend(head, 0, ROWS, keys, values, last=True)
         return carry
 
-    lax.fori_loop(0, heads, distant, 0)
+    lax.fori_loop(0, heads, level3, 0)
 
     for item in copies.values():
         item.wait_send()
@@ -242,9 +266,12 @@
     return pl.pallas_call(
         kernel,
         out_shape=jax.ShapeDtypeStruct((rows, width), BF16),
-        in_specs=[pl.BlockSpec(memory_space=pltpu.VMEM)] * 3,
+        in_specs=[pl.BlockSpec(memory_space=pltpu.HBM)] * 3,
         out_specs=pl.BlockSpec(memory_space=pltpu.VMEM),
         scratch_shapes=[
+            pltpu.VMEM((rows, width), BF16),
+            pltpu.VMEM((rows, width), BF16),
+            pltpu.VMEM((rows, width), BF16),
             pltpu.VMEM((2, 2, BLOCK, width), BF16),
             pltpu.VMEM((2, 256, width), BF16),
             pltpu.VMEM((2, 128, width), BF16),
@@ -254,16 +281,18 @@
             pltpu.VMEM((16, width), BF16),
             pltpu.VMEM((16, width), BF16),
             pltpu.VMEM((2, 128, width), BF16),
-            pltpu.VMEM((2, 2, 128, width), BF16),
+            pltpu.VMEM((2, 2, 64, width), BF16),
+            pltpu.VMEM((2, 2, 2, 32, width), BF16),
             pltpu.VMEM((2, 16, width), BF16),
             pltpu.VMEM((4, 16, width), BF16),
             pltpu.VMEM((2, 2, 4, PACK, width), BF16),
             state, state, state,
             pltpu.SemaphoreType.DMA((COPIES,)),
             pltpu.SemaphoreType.DMA((COPIES,)),
+            pltpu.SemaphoreType.DMA((3,)),
         ],
         compiler_params=pltpu.CompilerParams(
-            collective_id=0, has_side_effects=True, vmem_limit_bytes=48 * 1024 * 1024
+            collective_id=0, has_side_effects=True, vmem_limit_bytes=62 * 1024 * 1024
         ),
         name="hierarchical_attention",
     )(queries, keys, values)

time: 48.3 us -> 47.2 us (0.977)
  local copies, waits for them, and re-layouts: 4.65 us -> 2.26 us
  Pallas kernels: 43.4 us -> 44.7 us
    unnamed x7 -> x1, local copies, waits for them, and re-layouts: 4.65 us -> 2.26 us
    pallas_call x1, Pallas kernels: 43.4 us -> 44.7 us  [per_device(): pl.pallas_call(kernel, out_shape=jax.ShapeDtypeStruct((rows, width), BF16...]
where the time goes in v2:
time: 47.2 us; the launch traced here: 47 us
  Pallas kernels  44.7 us (95%)
  local copies, waits for them, and re-layouts  2.26 us (5%)
    pallas_call x1, Pallas kernels, per_device(): pl.pallas_call(kernel, out_shape=jax.ShapeDtypeStruct((rows, width), BF16...  44.7 us
    unnamed x1, local copies, waits for them, and re-layouts  2.26 us

profile of v2, /device:TPU:1, one launch (start us, length us, event | category | flops | bytes accessed | tf_op | source)
XLA Modules:
  0.0 47.0 jit_solution(10019905634670452331)
XLA Ops:
  0.0 44.7 %hierarchical_attention.1 = bf16[512,1024]{1,0:T(8,128)(2,1)} custom-call(bf16[512,1024]{1,0:T(8,128)(2,1)} %q_hbm.1, bf16[512,1024]{1,0:T(8,128)(2,1)} %k_hbm.1, bf16[512,1024]{1,0:T(8,128)(2,1)} %v_hbm.1), custom_call_target="tpu_custom_call" | custom-call | tf_op jit(solution)/shard_map/hierarchical_attention/pallas_call | solution.py:266
  44.8 2.3 %copy.5 = bf16[512,1024]{1,0:T(8,128)(2,1)} copy(bf16[512,1024]{1,0:T(8,128)(2,1)} %hierarchical_attention.1) | data formatting | bytes 2097152

commit v3 on v2

--- a/solution.py
+++ b/solution.py
@@ -125,7 +125,6 @@
     send(HALO + 2, k_hbm.at[head_rows], halo.at[0, 1], down)
     send(HALO + 3, v_hbm.at[head_rows], halo.at[1, 1], down)
     send(LEVEL2, c2, far2, twin)
-    send(LEVEL3, c3.at[0], far3.at[0, core], side_a)
 
     def attend(head, row, rows, keys, values, first=False, last=False, valid=None):
         lanes = pl.ds(pl.multiple_of(head * HEAD_DIM, HEAD_DIM), HEAD_DIM)
@@ -144,7 +143,10 @@
             old = peak[head, span]
             new = jnp.maximum(old, top)
             fade = jnp.exp2((old - new) * scale)
-        wide = jnp.concatenate([new] * (count // 128), axis=1)
+        spread = [new] * (count // 128)
+        if count % 128:
+            spread.append(new[:, :count % 128])
+        wide = jnp.concatenate(spread, axis=1)
         weights = jnp.exp2((scores - wide) * scale).astype(BF16)
         ones = jnp.ones((count, 128), BF16)
         both = jnp.dot(
@@ -175,7 +177,11 @@
         return carry
 
     loads[2].wait()
-    lax.fori_loop(0, heads, own, 0)
+    lax.fori_loop(0, heads // 2, own, 0)
+    copies[LEVEL4].wait_recv()
+    send(LEVEL4 + 1, far4.at[:, core, 0], far4.at[:, core, 1], side_a)
+    send(SHARE4, far4.at[:, core, 0], far4.at[:, core, 0], twin)
+    lax.fori_loop(heads // 2, heads, own, 0)
 
     for number in range(LEVEL5, LEVEL7 + 4):
         copies[number].wait_recv()
@@ -190,10 +196,8 @@
     send(ALONG_X, pack(x), pack(x), side_a)
     send(ALONG_X + 1, pack(x), pack(x), side_b)
     send(SHARE, pack(x), pack(x), twin)
-    copies[LEVEL4].wait_recv()
-    send(LEVEL4 + 1, far4.at[:, core, 0], far4.at[:, core, 1], side_a)
-    send(SHARE4, far4.at[:, core, 0], far4.at[:, core, 0], twin)
-    send(LEVEL3 + 1, c3.at[1], far3.at[1, core], side_a)
+    for which in range(2):
+        send(LEVEL3 + which, c3.at[which], far3.at[which, core], side_a)
 
     for number in range(HALO, LEVEL2 + 1):
         copies[number].wait_recv()
@@ -218,22 +222,16 @@
     send(SHARE + 2, pack(xb), pack(xb), twin)
     copies[LEVEL4 + 1].wait_recv()
     send(SHARE4 + 1, far4.at[:, core, 1], far4.at[:, core, 1], twin)
-    copies[ALONG_X + 2].wait_recv()
-    send(SHARE + 3, pack(xc), pack(xc), twin)
-    for number in (LEVEL3, LEVEL3 + 1):
-        copies[number].wait_recv()
-    send(SHARE3, far3.at[:, core], far3.at[:, core], twin)
-    for number in (SHARE4, SHARE4 + 1, SHARE, SHARE + 1, SHARE + 2, SHARE + 3):
-        copies[number].wait_recv()
-
-    def distant(head, carry):
+    for number in (SHARE4, SHARE4 + 1, SHARE, SHARE + 1):
+        copies[number].wait_recv()
+
+    def pair(place, rest, head, carry):
         lanes = lanes_of(head)
+        base = place - lax.rem(place, 2)
         keys, values = (
             jnp.concatenate(
-                [
-                    far567[which, :, :, :, lanes].reshape(8 * PACK, HEAD_DIM),
-                    far4[which, :, :, :, lanes].reshape(128, HEAD_DIM),
-                ],
+                [source[which, :, :, :, lanes].reshape(128, HEAD_DIM) for source in rest]
+                + [far567[which, :, pl.ds(base, 2), :, lanes].reshape(4 * PACK, HEAD_DIM)],
                 axis=0,
             )
             for which in range(2)
@@ -242,7 +240,18 @@
             attend(head, part * 256, 256, keys, values)
         return carry
 
-    lax.fori_loop(0, heads, distant, 0)
+    near_pair = functools.partial(pair, x, [far4])
+    lax.fori_loop(0, heads * 3 // 4, near_pair, 0)
+    copies[ALONG_X + 2].wait_recv()
+    send(SHARE + 3, pack(xc), pack(xc), twin)
+    lax.fori_loop(heads * 3 // 4, heads, near_pair, 0)
+
+    for number in (LEVEL3, LEVEL3 + 1):
+        copies[number].wait_recv()
+    send(SHARE3, far3.at[:, core], far3.at[:, core], twin)
+    for number in (SHARE + 2, SHARE + 3):
+        copies[number].wait_recv()
+    lax.fori_loop(0, heads, functools.partial(pair, xc, []), 0)
 
     copies[SHARE3].wait_recv()
 

time: 47.2 us -> 49.7 us (1.053)
  Pallas kernels: 44.7 us -> 47.3 us
    pallas_call x1, Pallas kernels: 44.7 us -> 47.3 us  [per_device(): pl.pallas_call(kernel, out_shape=jax.ShapeDtypeStruct((rows, width), BF16...]
where the time goes in v3:
time: 49.7 us; the launch traced here: 49.5 us
  Pallas kernels  47.3 us (95%)
  local copies, waits for them, and re-layouts  2.26 us (5%)
    pallas_call x1, Pallas kernels, per_device(): pl.pallas_call(kernel, out_shape=jax.ShapeDtypeStruct((rows, width), BF16...  47.3 us
    unnamed x1, local copies, waits for them, and re-layouts  2.26 us

profile of v3, /device:TPU:1, one launch (start us, length us, event | category | flops | bytes accessed | tf_op | source)
XLA Modules:
  0.0 49.5 jit_solution(17253712637564598125)
XLA Ops:
  0.0 47.3 %hierarchical_attention.1 = bf16[512,1024]{1,0:T(8,128)(2,1)} custom-call(bf16[512,1024]{1,0:T(8,128)(2,1)} %q_hbm.1, bf16[512,1024]{1,0:T(8,128)(2,1)} %k_hbm.1, bf16[512,1024]{1,0:T(8,128)(2,1)} %v_hbm.1), custom_call_target="tpu_custom_call" | custom-call | tf_op jit(solution)/shard_map/hierarchical_attention/pallas_call | solution.py:275
  47.3 2.3 %copy.5 = bf16[512,1024]{1,0:T(8,128)(2,1)} copy(bf16[512,1024]{1,0:T(8,128)(2,1)} %hierarchical_attention.1) | data formatting | bytes 2097152

commit v4 on v2

--- a/solution.py
+++ b/solution.py
@@ -1,4 +1,3 @@
-import functools
 import math
 
 import jax
@@ -125,7 +124,8 @@
     send(HALO + 2, k_hbm.at[head_rows], halo.at[0, 1], down)
     send(HALO + 3, v_hbm.at[head_rows], halo.at[1, 1], down)
     send(LEVEL2, c2, far2, twin)
-    send(LEVEL3, c3.at[0], far3.at[0, core], side_a)
+    for which in range(2):
+        send(LEVEL3 + which, c3.at[which], far3.at[which, core], side_a)
 
     def attend(head, row, rows, keys, values, first=False, last=False, valid=None):
         lanes = pl.ds(pl.multiple_of(head * HEAD_DIM, HEAD_DIM), HEAD_DIM)
@@ -175,7 +175,11 @@
         return carry
 
     loads[2].wait()
-    lax.fori_loop(0, heads, own, 0)
+    lax.fori_loop(0, heads // 2, own, 0)
+    copies[LEVEL4].wait_recv()
+    send(LEVEL4 + 1, far4.at[:, core, 0], far4.at[:, core, 1], side_a)
+    send(SHARE4, far4.at[:, core, 0], far4.at[:, core, 0], twin)
+    lax.fori_loop(heads // 2, heads, own, 0)
 
     for number in range(LEVEL5, LEVEL7 + 4):
         copies[number].wait_recv()
@@ -190,10 +194,6 @@
     send(ALONG_X, pack(x), pack(x), side_a)
     send(ALONG_X + 1, pack(x), pack(x), side_b)
     send(SHARE, pack(x), pack(x), twin)
-    copies[LEVEL4].wait_recv()
-    send(LEVEL4 + 1, far4.at[:, core, 0], far4.at[:, core, 1], side_a)
-    send(SHARE4, far4.at[:, core, 0], far4.at[:, core, 0], twin)
-    send(LEVEL3 + 1, c3.at[1], far3.at[1, core], side_a)
 
     for number in range(HALO, LEVEL2 + 1):
         copies[number].wait_recv()
@@ -218,20 +218,18 @@
     send(SHARE + 2, pack(xb), pack(xb), twin)
     copies[LEVEL4 + 1].wait_recv()
     send(SHARE4 + 1, far4.at[:, core, 1], far4.at[:, core, 1], twin)
-    copies[ALONG_X + 2].wait_recv()
-    send(SHARE + 3, pack(xc), pack(xc), twin)
     for number in (LEVEL3, LEVEL3 + 1):
         copies[number].wait_recv()
     send(SHARE3, far3.at[:, core], far3.at[:, core], twin)
-    for number in (SHARE4, SHARE4 + 1, SHARE, SHARE + 1, SHARE + 2, SHARE + 3):
-        copies[number].wait_recv()
-
-    def distant(head, carry):
+    for number in (SHARE4, SHARE4 + 1, SHARE3):
+        copies[number].wait_recv()
+
+    def middle(head, carry):
         lanes = lanes_of(head)
         keys, values = (
             jnp.concatenate(
                 [
-                    far567[which, :, :, :, lanes].reshape(8 * PACK, HEAD_DIM),
+                    far3[which, :, :, lanes].reshape(128, HEAD_DIM),
                     far4[which, :, :, :, lanes].reshape(128, HEAD_DIM),
                 ],
                 axis=0,
@@ -242,18 +240,23 @@
             attend(head, part * 256, 256, keys, values)
         return carry
 
+    lax.fori_loop(0, heads // 2, middle, 0)
+    copies[ALONG_X + 2].wait_recv()
+    send(SHARE + 3, pack(xc), pack(xc), twin)
+    lax.fori_loop(heads // 2, heads, middle, 0)
+
+    for number in range(SHARE, SHARE + 4):
+        copies[number].wait_recv()
+
+    def distant(head, carry):
+        lanes = lanes_of(head)
+        keys = far567[0, :, :, :, lanes].reshape(8 * PACK, HEAD_DIM)
+        values = far567[1, :, :, :, lanes].reshape(8 * PACK, HEAD_DIM)
+        for part in range(2):
+            attend(head, part * 256, 256, keys, values, last=True)
+        return carry
+
     lax.fori_loop(0, heads, distant, 0)
-
-    copies[SHARE3].wait_recv()
-
-    def level3(head, carry):
-        lanes = lanes_of(head)
-        keys = far3[0, :, :, lanes].reshape(128, HEAD_DIM)
-        values = far3[1, :, :, lanes].reshape(128, HEAD_DIM)
-        attend(head, 0, ROWS, keys, values, last=True)
-        return carry
-
-    lax.fori_loop(0, heads, level3, 0)
 
     for item in copies.values():
         item.wait_send()

time: 47.2 us -> 43.7 us (0.926)
  Pallas kernels: 44.7 us -> 41.3 us
    pallas_call x1, Pallas kernels: 44.7 us -> 41.3 us  [per_device(): pl.pallas_call(kernel, out_shape=jax.ShapeDtypeStruct((rows, width), BF16...]
where the time goes in v4:
time: 43.7 us; the launch traced here: 43.6 us
  Pallas kernels  41.3 us (95%)
  local copies, waits for them, and re-layouts  2.26 us (5%)
    pallas_call x1, Pallas kernels, per_device(): pl.pallas_call(kernel, out_shape=jax.ShapeDtypeStruct((rows, width), BF16...  41.3 us
    unnamed x1, local copies, waits for them, and re-layouts  2.26 us

profile of v4, /device:TPU:1, one launch (start us, length us, event | category | flops | bytes accessed | tf_op | source)
XLA Modules:
  0.0 43.6 jit_solution(15101398550444102829)
XLA Ops:
  0.0 41.3 %hierarchical_attention.1 = bf16[512,1024]{1,0:T(8,128)(2,1)} custom-call(bf16[512,1024]{1,0:T(8,128)(2,1)} %q_hbm.1, bf16[512,1024]{1,0:T(8,128)(2,1)} %k_hbm.1, bf16[512,1024]{1,0:T(8,128)(2,1)} %v_hbm.1), custom_call_target="tpu_custom_call" | custom-call | tf_op jit(solution)/shard_map/hierarchical_attention/pallas_call | solution.py:269
  41.3 2.3 %copy.5 = bf16[512,1024]{1,0:T(8,128)(2,1)} copy(bf16[512,1024]{1,0:T(8,128)(2,1)} %hierarchical_attention.1) | data formatting | bytes 2097152
